TPU v7x, 32 devices: a whole 2x2x4 slice. The times are simulated.
32 devices in a mesh: seq: 8 (over z, x), hid: 4 (over y, core).
Axes of the slice: x: 2, y: 2, z: 4, core: 2. Of those that a mesh axis runs over, the one named last changes fastest.
Arguments:
- tokens: bfloat16 [1024, 4096], P('seq', 'hid'), may hold values from -6 to 6
- hidden_grad: bfloat16 [1024, 14336], P('seq', 'hid'), may hold values from -6 to 6
- gate_blocks: bfloat16 [4, 448, 128, 128], P('hid', 'seq'), may hold values from -0.125 to 0.125
- up_blocks: bfloat16 [4, 448, 128, 128], P('hid', 'seq'), may hold values from -0.125 to 0.125
- gate_rows: int32 [4, 448], P('hid'), may hold values from 0 to 31, as said below
- gate_cols: int32 [4, 448], P('hid'), may hold values from 0 to 27
- gate_count: int32 [4], P('hid'), may hold values from 56 to 448, as said below
- up_rows: int32 [4, 448], P('hid'), may hold values from 0 to 31, as said below
- up_cols: int32 [4, 448], P('hid'), may hold values from 0 to 27
- up_count: int32 [4], P('hid'), may hold values from 56 to 448, as said below
Outputs:
- hidden: bfloat16 [1024, 14336], P('seq', 'hid')
- input_grad: bfloat16 [1024, 4096], P('seq', 'hid')
- gate_block_grads: bfloat16 [4, 448, 128, 128], P('hid', 'seq')
- up_block_grads: bfloat16 [4, 448, 128, 128], P('hid', 'seq')
Inputs may be any that keep to these rules, and one draw needn't show every extreme that they name: For each panel, the pairs (gate_rows, gate_cols) over all 448 slots are distinct. `gate_count`: slots at or after a panel's count hold no block of the matrix. For each panel, the pairs (up_rows, up_cols) over all 448 slots are distinct. `up_count`: slots at or after a panel's count hold no block of the matrix.
All inputs are finite; a program needn't handle non-finite values.
Results may differ from a plain program's by a relative error of at most 0.018.
Values may be sent and summed in bfloat16 or wider, within the bound.
A program may use at most 192 MiB of HBM per device.

v0:
```python
import math

import jax
import jax.numpy as jnp
from jax import lax
from jax.sharding import PartitionSpec as P


def swapped(value, axis, stride):
    mask = 2**stride
    pairs = [(source, source ^ mask) for source in range(lax.axis_size(axis))]
    return lax.ppermute(value, axis, pairs)


def silu_parts(preact):
    sigma = jax.nn.sigmoid(preact)
    return (preact * sigma, sigma * (1.0 + preact * (1.0 - sigma)))


def place_split(products, placing, form):
    high_part = products.astype(jnp.bfloat16)
    rest_part = (products - high_part.astype(jnp.float32)).astype(jnp.bfloat16)
    table = placing.astype(jnp.bfloat16)
    placed = jnp.einsum(form, high_part, table, preferred_element_type=jnp.float32)
    return placed + jnp.einsum(form, rest_part, table, preferred_element_type=jnp.float32)


def project_slots(tiles, weights, rows, columns, live_count, group_size, trips, col_blocks):
    tok_rows = tiles.shape[0]
    block_size = tiles.shape[2]
    targets = jnp.arange(col_blocks)
    offsets = jnp.arange(group_size)

    def project_one_group(group_index, running):
        start = group_index * group_size
        chosen = lax.dynamic_slice_in_dim(weights, start, group_size, 0)
        row_ids = lax.dynamic_slice_in_dim(rows, start, group_size, 0)
        col_ids = lax.dynamic_slice_in_dim(columns, start, group_size, 0)
        active = start + offsets < live_count
        picked = jnp.take(tiles, row_ids, axis=1)
        products = jnp.einsum("tsk,skn->tsn", picked, chosen, preferred_element_type=jnp.float32)
        placing = (col_ids[:, None] == targets[None, :]) & active[:, None]
        return running + place_split(products, placing, "tsn,sc->tcn")

    initial = jnp.zeros((tok_rows, col_blocks, block_size), jnp.float32)
    return lax.fori_loop(0, trips, project_one_group, initial)


def return_slots(grad_tiles, weights, rows, columns, live_count, group_size, trips, row_blocks):
    tok_rows = grad_tiles.shape[0]
    block_size = grad_tiles.shape[2]
    targets = jnp.arange(row_blocks)
    offsets = jnp.arange(group_size)

    def return_one_group(group_index, running):
        start = group_index * group_size
        chosen = lax.dynamic_slice_in_dim(weights, start, group_size, 0)
        row_ids = lax.dynamic_slice_in_dim(rows, start, group_size, 0)
        col_ids = lax.dynamic_slice_in_dim(columns, start, group_size, 0)
        active = start + offsets < live_count
        picked = jnp.take(grad_tiles, col_ids, axis=1)
        products = jnp.einsum("tsn,skn->tsk", picked, chosen, preferred_element_type=jnp.float32)
        placing = (row_ids[:, None] == targets[None, :]) & active[:, None]
        return running + place_split(products, placing, "tsk,sr->trk")

    initial = jnp.zeros((tok_rows, row_blocks, block_size), jnp.float32)
    return lax.fori_loop(0, trips, return_one_group, initial)


def on_device(
    tokens,
    hidden_grad,
    gate_blocks,
    up_blocks,
    gate_rows,
    gate_cols,
    gate_count,
    up_rows,
    up_cols,
    up_count,
):
    gathered = lax.all_gather(tokens, "hid", axis=1, tiled=True)
    tok_rows = gathered.shape[0]
    block_size = gate_blocks.shape[2]
    row_blocks = gathered.shape[1] // block_size
    col_blocks = hidden_grad.shape[1] // block_size
    gate_all = lax.all_gather(gate_blocks, "seq", axis=1, tiled=True)
    up_all = lax.all_gather(up_blocks, "seq", axis=1, tiled=True)
    capacity = gate_all.shape[1]
    group_size = 32
    groups = capacity // group_size
    gate_live = gate_count[0]
    up_live = up_count[0]
    tiles = gathered.reshape(tok_rows, row_blocks, block_size)
    gate_pre = project_slots(
        tiles, gate_all[0], gate_rows[0], gate_cols[0], gate_live, group_size, groups, col_blocks
    )
    up_pre = project_slots(
        tiles, up_all[0], up_rows[0], up_cols[0], up_live, group_size, groups, col_blocks
    )
    activated, slope = silu_parts(gate_pre)
    hidden = (activated * up_pre).astype(jnp.bfloat16)
    upstream = hidden_grad.reshape(tok_rows, col_blocks, block_size).astype(jnp.float32)
    gate_grad = (upstream * up_pre * slope).astype(jnp.bfloat16)
    up_grad = (upstream * activated).astype(jnp.bfloat16)
    input_sum = return_slots(
        gate_grad,
        gate_all[0],
        gate_rows[0],
        gate_cols[0],
        gate_live,
        group_size,
        groups,
        row_blocks,
    )
    input_sum = input_sum + return_slots(
        up_grad, up_all[0], up_rows[0], up_cols[0], up_live, group_size, groups, row_blocks
    )
    input_grad = lax.psum_scatter(
        input_sum.reshape(tok_rows, row_blocks * block_size).astype(jnp.bfloat16),
        "hid",
        scatter_dimension=1,
        tiled=True,
    )
    seq_count = lax.axis_size("seq")
    position = lax.axis_index("seq")
    levels = seq_count.bit_length() - 1
    blk_dev = capacity // seq_count
    other_tiles, other_gate, other_up = swapped((tiles, gate_grad, up_grad), "seq", 0)
    both_tiles = jnp.concatenate([tiles, other_tiles], axis=0)
    both_gate = jnp.concatenate([gate_grad, other_gate], axis=0)
    both_up = jnp.concatenate([up_grad, other_up], axis=0)
    parity = position % 2
    owners = 2 * jnp.arange(seq_count // 2) + parity
    slot_ids = (owners[:, None] * blk_dev + jnp.arange(blk_dev)[None, :]).reshape(-1)
    stacked = []
    for rows, columns, live_count, grad_tiles in (
        (gate_rows[0], gate_cols[0], gate_live, both_gate),
        (up_rows[0], up_cols[0], up_live, both_up),
    ):
        row_ids = jnp.take(rows, slot_ids)
        col_ids = jnp.take(columns, slot_ids)
        picked_input = jnp.take(both_tiles, row_ids, axis=1)
        picked_grad = jnp.take(grad_tiles, col_ids, axis=1)
        block_term = jnp.einsum(
            "tsk,tsn->skn", picked_input, picked_grad, preferred_element_type=jnp.float32
        )
        stacked.append(block_term * (slot_ids < live_count).astype(jnp.float32)[:, None, None])
    current = jnp.stack(stacked, axis=1)
    current = current.reshape((seq_count // 2, blk_dev) + current.shape[1:])
    for level in range(1, levels):
        own_bit = position // 2**level % 2
        halves = current.reshape((current.shape[0] // 2, 2) + current.shape[1:])
        kept = lax.dynamic_index_in_dim(halves, own_bit, 1, keepdims=False)
        sent = lax.dynamic_index_in_dim(halves, 1 - own_bit, 1, keepdims=False)
        received = swapped(sent.astype(jnp.bfloat16), "seq", level)
        current = kept + received.astype(jnp.float32)
    summed = current[0]
    scale = 1.0 / math.sqrt(tok_rows * seq_count)
    gate_block_grads = (summed[:, 0] * scale).astype(jnp.bfloat16)[None]
    up_block_grads = (summed[:, 1] * scale).astype(jnp.bfloat16)[None]
    return (
        hidden.reshape(tok_rows, col_blocks * block_size),
        input_grad,
        gate_block_grads,
        up_block_grads,
    )


def solution(mesh):
    placed = (
        P("seq", "hid"),
        P("seq", "hid"),
        P("hid", "seq", None, None),
        P("hid", "seq", None, None),
        P("hid", None),
        P("hid", None),
        P("hid"),
        P("hid", None),
        P("hid", None),
        P("hid"),
    )
    return jax.shard_map(
        on_device,
        mesh=mesh,
        in_specs=placed,
        out_specs=(
            P("seq", "hid"),
            P("seq", "hid"),
            P("hid", "seq", None, None),
            P("hid", "seq", None, None),
        ),
        check_vma=False,
    )
```

profile of v0, /device:TPU:0, one launch (start us, length us, event | category | flops | bytes accessed | tf_op | source)
XLA Modules:
  0.0 1165.4 jit_solution(1844786483724718215)
XLA Ops:
  16.3 13.3 %all-gather.6.cloned.1.call-done = bf16[128,4096]{0,1:T(8,128)(2,1)} async-done(((bf16[128,1024]{0,1:T(8,128)(2,1)}), bf16[128,4096]{0,1:T(8,128)(2,1)}) %all-gather.6.cloned.1.call-update) | async-done | bytes 1048592 | tf_op jit(solution)/shard_map/all_gather | solution.py:82
  33.3 200.2 %all-gather.8.cloned.1.call-done = bf16[1,448,128,128]{3,2,0,1:T(8,128)(2,1)} async-done(((bf16[1,56,128,128]{3,2,0,1:T(8,128)(2,1)}), bf16[1,448,128,128]{3,2,0,1:T(8,128)(2,1)}) %all-gather.8.cloned.1.call-update) | async-done | bytes 14680080 | tf_op jit(solution)/shard_map/all_gather | solution.py:88
  233.5 192.3 %while.61 = (s32[]{:T(128)}, f32[128,28,128]{2,1,0:T(8,128)}, s32[448]{0:T(512)S(1)}, s32[]{:T(128)}, bf16[448,128,128]{2,1,0:T(8,128)(2,1)}, /*index=5*/s32[448...) while((s32[]{:T(128)}, f32[128,28,128]{2,1,0:T(8,128)}, ...), condition=%wide.region_3.5_spmd.clone, body=%wide.region_2.4_spmd.clone.sunk | while | flops 196940544 | bytes 19928416 | solution.py:46
  256.7 3.7 bitcast_add_fusion.9
  284.1 3.7 bitcast_add_fusion.9
  311.5 4.6 bitcast_add_fusion.9
  326.1 3.7 bitcast_add_fusion.9
  353.5 3.7 bitcast_add_fusion.9
  394.6 3.9 bitcast_add_fusion.9
  425.8 9.8 all-gather.4.cloned.1.call-done
  435.6 193.2 %while.60 = (s32[]{:T(128)}, f32[128,28,128]{2,1,0:T(8,128)}, s32[448]{0:T(512)S(1)}, s32[]{:T(128)}, bf16[448,128,128]{2,1,0:T(8,128)(2,1)}, /*index=5*/s32[448...) while((s32[]{:T(128)}, f32[128,28,128]{2,1,0:T(8,128)}, ...), condition=%wide.region_1.3_spmd.clone, body=%wide.region_0.2_spmd.clone.sunk | while | flops 196940544 | bytes 19928416 | solution.py:46
  458.7 3.8 bitcast_add_fusion.8
  472.6 3.8 bitcast_add_fusion.8
  486.4 3.8 bitcast_add_fusion.8
  500.3 3.8 bitcast_add_fusion.8
  514.2 3.8 bitcast_add_fusion.8
  528.0 3.8 bitcast_add_fusion.8
  541.9 3.8 bitcast_add_fusion.8
  555.7 3.8 bitcast_add_fusion.8
  569.6 3.8 bitcast_add_fusion.8
  583.4 3.8 bitcast_add_fusion.8
  597.3 3.8 bitcast_add_fusion.8
  611.1 3.8 bitcast_add_fusion.8
  625.0 3.8 bitcast_add_fusion.8
  628.8 6.5 multiply_convert_fusion.1
  645.1 9.4 gather_fusion.5
  654.5 9.2 gather_fusion.9
  665.3 9.2 gather_fusion.7
  678.0 9.1 gather_fusion.11
  687.2 18.4 %fusion.105 = f32[224,128,128]{2,1,0:T(8,128)} fusion(bf16[224,256,128]{2,1,0:T(8,128)(2,1)} %gather_fusion.7, pred[224]{0:T(512)(128)(4,1)S(1)} %get-tuple-element.961, bf16[224,256,128]{2,1,0:T(8,128)(2,1)} %gather_fusion.5, pred[224]{0:T(512)(128)(4,1)S(1)} %get-tuple-element.963, f32[224]{0:T(256)S(1)} %get-tuple-element.960), kind=kOutput, calls=%fused_computation.141 | convolution fusion | flops 1897398272 | bytes 44041536 | tf_op jit(solution)/shard_map/tsk,tsn->skn/dot_general | solution.py:145
  705.6 18.5 %fusion.110 = f32[224,128,128]{2,1,0:T(8,128)} fusion(bf16[224,256,128]{2,1,0:T(8,128)(2,1)} %gather_fusion.11, pred[224]{0:T(512)(128)(4,1)S(1)} %get-tuple-element.944, bf16[224,256,128]{2,1,0:T(8,128)(2,1)} %gather_fusion.9, pred[224]{0:T(512)(128)(4,1)S(1)} %get-tuple-element.941, f32[224]{0:T(256)S(1)} %get-tuple-element.959), kind=kOutput, calls=%fused_computation.142 | convolution fusion | flops 1897398272 | bytes 44041536 | tf_op jit(solution)/shard_map/tsk,tsn->skn/dot_general | solution.py:145
  724.1 10.1 fusion.115
  734.2 192.1 %while.62 = (s32[]{:T(128)}, f32[128,32,128]{2,1,0:T(8,128)}, s32[448]{0:T(512)S(1)}, s32[]{:T(128)}, bf16[448,128,128]{2,1,0:T(8,128)(2,1)}, /*index=5*/s32[448...) while((s32[]{:T(128)}, f32[128,32,128]{2,1,0:T(8,128)}, ...), condition=%wide.region_5.8_spmd.clone.clone, body=%wide.region_4.0_spmd.clone.clone.sunk | while | flops 205526272 | bytes 20976992 | solution.py:67
  757.1 3.9 bitcast_add_fusion.10
  770.9 3.9 bitcast_add_fusion.10
  784.7 3.9 bitcast_add_fusion.10
  798.4 3.9 bitcast_add_fusion.10
  812.2 3.9 bitcast_add_fusion.10
  826.0 3.9 bitcast_add_fusion.10
  839.8 3.9 bitcast_add_fusion.10
  853.5 3.9 bitcast_add_fusion.10
  867.3 3.9 bitcast_add_fusion.10
  881.1 3.9 bitcast_add_fusion.10
  894.8 3.9 bitcast_add_fusion.10
  908.6 3.9 bitcast_add_fusion.10
  922.4 3.9 bitcast_add_fusion.10
  926.2 8.6 fusion.90
  934.9 5.1 copy-done.7
  945.5 186.0 %while.63 = (s32[]{:T(128)}, f32[128,32,128]{2,1,0:T(8,128)}, s32[448]{0:T(512)}, s32[]{:T(128)}, bf16[448,128,128]{2,1,0:T(8,128)(2,1)}, /*index=5*/s32[448]{0:...) while((s32[]{:T(128)}, f32[128,32,128]{2,1,0:T(8,128)}, ...), condition=%wide.region_7.10_spmd.clone.clone, body=%wide.region_6.9_spmd.clone.clone.sunk | while | flops 205526272 | bytes 24647044 | solution.py:67
  967.5 3.9 bitcast_add_fusion.11
  980.9 3.9 bitcast_add_fusion.11
  994.2 3.9 bitcast_add_fusion.11
  1007.5 3.9 bitcast_add_fusion.11
  1020.9 3.9 bitcast_add_fusion.11
  1034.2 3.9 bitcast_add_fusion.11
  1047.5 3.9 bitcast_add_fusion.11
  1060.8 3.9 bitcast_add_fusion.11
  1074.2 3.9 bitcast_add_fusion.11
  1087.5 3.9 bitcast_add_fusion.11
  1100.8 3.9 bitcast_add_fusion.11
  1114.2 3.9 bitcast_add_fusion.11
  1127.5 3.9 bitcast_add_fusion.11
  1137.6 5.8 add_bitcast_fusion
  1146.2 12.6 %reduce-scatter.2.cloned.1.call-done = bf16[128,1024]{1,0:T(8,128)(2,1)} async-done(((bf16[128,4096]{1,0:T(8,128)(2,1)}), bf16[128,1024]{1,0:T(8,128)(2,1)}) %reduce-scatter.2.cloned.1.call-update) | async-done | bytes 262160 | tf_op jit(solution)/shard_map/reduce_scatter | solution.py:119
  (553 shorter events, 628.1 us)
Async XLA Ops:
  7.2 22.4 %all-gather.6.cloned.1.call-start = ((), (), s32[]{:S(2)}) async-start(), calls=%async_computation.2 | async-start | bytes 1310720 | tf_op jit(solution)/shard_map/all_gather | solution.py:82
  9.0 1.6 copy-start.9
  9.0 224.4 %all-gather.8.cloned.1.call-start = ((), (), s32[]{:S(2)}) async-start(), calls=%async_computation.3 | async-start | bytes 16515072 | tf_op jit(solution)/shard_map/all_gather | solution.py:88
  9.8 425.8 %all-gather.4.cloned.1.call-start = ((), (), s32[]{:S(2)}) async-start(), calls=%async_computation.1 | async-start | bytes 16515072 | tf_op jit(solution)/shard_map/all_gather | solution.py:87
  10.5 1148.3 %reduce-scatter.2.cloned.1.call-start = ((), (), s32[]{:S(2)}) async-start(), calls=%async_computation.4 | async-start | bytes 1310720 | tf_op jit(solution)/shard_map/reduce_scatter | solution.py:119
  10.6 3.7 copy-start.3
  12.8 220.6 %copy-start.2 = (s32[1,448]{1,0:T(1,128)S(1)}, s32[1,448]{1,0:T(1,128)}, u32[]{:S(2)}) copy-start(s32[1,448]{1,0:T(1,128)} %param.36) | copy-start | bytes 5380
  31.8 611.6 %collective-permute-start = (bf16[128,32,128]{2,0,1:T(8,128)(2,1)}, bf16[128,32,128]{2,0,1:T(8,128)(2,1)}, u32[]{:S(2)}, u32[]{:S(2)}) collective-permute-start(bf16[128,32,128]{2,0,1:T(8,128)(2,1)} %copy.98), channel_id=1, source_target_pairs={{0,4},{4,0},{8,12},{12,8},{16,20},{20,16},{24,28},{28,24},{1,5},{5... | collective-permute-start | bytes 3145736 | tf_op jit(solution)/shard_map/ppermute | solution.py:12
  233.5 202.1 %copy-start = (s32[1,448]{1,0:T(1,128)S(1)}, s32[1,448]{1,0:T(1,128)}, u32[]{:S(2)}) copy-start(s32[1,448]{1,0:T(1,128)} %param.33) | copy-start | bytes 5380
  233.5 202.1 %copy-start.1 = (s32[1,448]{1,0:T(1,128)S(1)}, s32[1,448]{1,0:T(1,128)}, u32[]{:S(2)}) copy-start(s32[1,448]{1,0:T(1,128)} %param.32) | copy-start | bytes 5380
  635.3 41.4 %copy-start.4 = (bf16[128,28,128]{2,0,1:T(8,128)(2,1)}, bf16[128,28,128]{2,0,1:T(8,128)(2,1)S(1)}, u32[]{:S(2)}) copy-start(bf16[128,28,128]{2,0,1:T(8,128)(2,1)S(1)} %get-tuple-element.1284) | copy-start | bytes 2752516
  635.3 28.4 %collective-permute-start.1 = (bf16[128,28,128]{2,0,1:T(8,128)(2,1)}, bf16[128,28,128]{2,0,1:T(8,128)(2,1)}, u32[]{:S(2)}, u32[]{:S(2)}) collective-permute-start(bf16[128,28,128]{2,0,1:T(8,128)(2,1)} %get-tuple-element.1251), channel_id=1, source_target_pairs={{0,4},{4,0},{8,12},{12,8},{16,20},{20,16},{24,28},{28,24},{1,5},{5... | collective-permute-start | bytes 2752520 | tf_op jit(solution)/shard_map/ppermute | solution.py:12
  635.9 40.8 %collective-permute-start.2 = (bf16[128,28,128]{2,0,1:T(8,128)(2,1)S(1)}, bf16[128,28,128]{2,0,1:T(8,128)(2,1)}, u32[]{:S(2)}, u32[]{:S(2)}) collective-permute-start(bf16[128,28,128]{2,0,1:T(8,128)(2,1)S(1)} %get-tuple-element.1284), channel_id=1, source_target_pairs={{0,4},{4,0},{8,12},{12,8},{16,20},{20,16},{24,28},{28,24},{1,5},{5... | collective-permute-start | bytes 2752520 | tf_op jit(solution)/shard_map/ppermute | solution.py:12
  734.2 192.1 %collective-permute-start.3 = (bf16[2,56,2,128,128]{4,3,1,2,0:T(8,128)(2,1)}, bf16[2,56,2,128,128]{4,3,1,2,0:T(8,128)(2,1)}, u32[]{:S(2)}, u32[]{:S(2)}) collective-permute-start(bf16[2,56,2,128,128]{4,3,1,2,0:T(8,128)(2,1)} %fusion.115), channel_id=1, source_target_pairs={{0,8},{4,12},{8,0},{12,4},{16,24},{20,28},{24,16},{28,20},{1,9},{5... | collective-permute-start | bytes 22020104 | tf_op jit(solution)/shard_map/ppermute | solution.py:12
  934.9 5.1 copy-start.7
  940.0 5.5 copy-start.5
  942.7 194.9 %collective-permute-start.4 = (bf16[1,56,2,128,128]{4,3,1,2,0:T(8,128)(2,1)}, bf16[1,56,2,128,128]{4,3,1,2,0:T(8,128)(2,1)}, u32[]{:S(2)}, u32[]{:S(2)}) collective-permute-start(bf16[1,56,2,128,128]{4,3,1,2,0:T(8,128)(2,1)} %dynamic-slice_convert_fusion), channel_id=1, source_target_pairs={{0,16},{4,20},{8,24},{12,28},{16,0},{20,4},{24,8},{28,12},{1,17},{... | collective-permute-start | bytes 11010056 | tf_op jit(solution)/shard_map/ppermute | solution.py:12
  954.9 3.3 copy-start.6
  967.5 3.9 copy-start.6
  980.9 3.9 copy-start.6
  994.2 3.9 copy-start.6
  1007.5 3.9 copy-start.6
  1020.9 3.9 copy-start.6
  1034.2 3.9 copy-start.6
  1047.5 3.9 copy-start.6
  1060.8 3.9 copy-start.6
  1074.2 3.9 copy-start.6
  1087.5 3.9 copy-start.6
  1100.8 3.9 copy-start.6
  1114.2 3.9 copy-start.6
  1127.5 3.9 copy-start.6
  1134.1 1.5 copy-start.8
Sparse Core Ops, SparseCore 0:
  10.1 19.4 all-gather.5
  31.8 201.6 all-gather.7
  235.7 199.8 all-gather.3
  1135.7 23.0 reduce-scatter.1
where the time goes:
time: 1170 us
  matrix products  461 us (39%)
  local copies, waits for them, and re-layouts  359 us (31%)
  waiting for transfers between devices  240 us (21%)
  other arithmetic  82.2 us (7%)
  between operations  15.4 us (1%)
    dot_general x56, matrix products, place_split(): jnp.einsum(form, rest_part, table, preferred_element_type=jnp.float32)  213 us
    all_gather x1, waiting for transfers between devices, on_device(): up_all = lax.all_gather(up_blocks, 'seq', axis=1, tiled=True)  200 us
    convert_element_type x56, local copies, waits for them, and re-layouts, place_split(): high_part = products.astype(jnp.bfloat16)  95.1 us
    convert_element_type x56, local copies, waits for them, and re-layouts, place_split(): rest_part = (products - high_part.astype(jnp.float32)).astype(jnp.bfloat16)  95.1 us
    dot_general x56, matrix products, place_split(): jnp.einsum(form, high_part, table, preferred_element_type=jnp.float32)  91.5 us
    dot_general x28, matrix products, return_one_group(): jnp.einsum('tsn,skn->tsk', picked, chosen, preferred_element_type=jnp.flo...  60.6 us
    dot_general x28, matrix products, project_one_group(): jnp.einsum('tsk,skn->tsn', picked, chosen, preferred_element_type=jnp.flo...  59.6 us
    gather x28, local copies, waits for them, and re-layouts, project_one_group(): picked = jnp.take(tiles, row_ids, axis=1)  55.3 us
  transfers between devices with their start and end apart: 9, of which 5 were waited for; matrix products, arithmetic and copies ran while one was open for 71% of the time, Pallas kernels for 0%

commit v1 on v0

v1 whole, which is shorter than its diff:
```python
import functools
import math

import jax
import jax.numpy as jnp
from jax import lax
from jax.experimental import pallas as pl
from jax.experimental.pallas import tpu as pltpu
from jax.sharding import Mesh, PartitionSpec as P

F32 = jnp.float32
BF16 = jnp.bfloat16
VMEM = pltpu.VMEM
SMEM = pltpu.SMEM
LIMIT = 66000000


def lanes(index, block):
    return pl.ds(pl.multiple_of(index * block, block), block)


def each_group(live, unroll, body):
    lax.fori_loop(0, (live + unroll - 1) // unroll, lambda i, c: (body(i * unroll), c)[1], 0)


def forward_kernel(own, block, per, unroll, base_ref, live_ref, rows_ref, cols_ref, tok_ref, mine_ref, other_ref, out_ref, acc):
    zc, tok_rows = tok_ref.shape[0], tok_ref.shape[2]
    spare = acc.shape[-1] // block - 1
    acc[...] = jnp.zeros_like(acc)
    for half, w_ref in enumerate((mine_ref, other_ref)):
        base = base_ref[half]
        live = jnp.clip(live_ref[0] - base, 0, own)

        def body(start, base=base, w_ref=w_ref, live=live):
            parts = []
            for u in range(unroll):
                row = rows_ref[0, base + start + u]
                x = tok_ref[:, row // per, :, lanes(row % per, block)]
                prod = jnp.dot(x.reshape(zc * tok_rows, block), w_ref[start + u], preferred_element_type=F32)
                parts.append(prod)
            for u, prod in enumerate(parts):
                col = jnp.where(start + u < live, cols_ref[0, base + start + u], spare)
                acc[:, lanes(col, block)] += prod

        each_group(live, unroll, body)
    for z in range(zc):
        out_ref[z] = acc[z * tok_rows : (z + 1) * tok_rows, : spare * block].astype(BF16)


def input_kernel(own, block, unroll, first, base_ref, live_ref, rows_ref, cols_ref, grad_ref, mine_ref, other_ref, *rest):
    prev_ref = None if first else rest[0]
    out_ref, acc = rest[-2:]
    zc, tok_rows = grad_ref.shape[0], grad_ref.shape[1]
    hs, width = out_ref.shape[0], out_ref.shape[3]
    spare = acc.shape[-1] // block - 1
    if first:
        acc[...] = jnp.zeros_like(acc)
    else:
        for h in range(hs):
            for z in range(zc):
                acc[z * tok_rows : (z + 1) * tok_rows, h * width : (h + 1) * width] = prev_ref[h, z]
    for half, w_ref in enumerate((mine_ref, other_ref)):
        base = base_ref[half]
        live = jnp.clip(live_ref[0] - base, 0, own)

        def body(start, base=base, w_ref=w_ref, live=live):
            parts = []
            for u in range(unroll):
                x = grad_ref[:, :, lanes(cols_ref[0, base + start + u], block)].reshape(zc * tok_rows, block)
                prod = lax.dot_general(x, w_ref[start + u], (((1,), (1,)), ((), ())), preferred_element_type=F32)
                parts.append(prod)
            for u, prod in enumerate(parts):
                row = jnp.where(start + u < live, rows_ref[0, base + start + u], spare)
                acc[:, lanes(row, block)] += prod

        each_group(live, unroll, body)
    for h in range(hs):
        for z in range(zc):
            piece = acc[z * tok_rows : (z + 1) * tok_rows, h * width : (h + 1) * width]
            out_ref[h, z] = piece.astype(out_ref.dtype)


def flip_kernel(block, per, tok_ref, out_ref):
    zc, hs, tok_rows = tok_ref.shape[0], tok_ref.shape[1], tok_ref.shape[2]

    def flip(row, carry):
        x = tok_ref[:, row // per, :, lanes(row % per, block)]
        out_ref[0, row] = x.reshape(zc * tok_rows, block).T
        return carry

    lax.fori_loop(0, hs * per, flip, 0)


def weight_kernel(own, block, unroll, steps, half, base_ref, live_ref, rows_ref, cols_ref, flip_ref, grad_ref, out_ref, acc):
    zc, tok_rows = grad_ref.shape[0], grad_ref.shape[1]
    base = base_ref[half]
    live = jnp.clip(live_ref[0] - base, 0, own)
    step = pl.program_id(0)

    def body(start):
        for u in range(unroll):
            row = rows_ref[0, base + start + u]
            col = cols_ref[0, base + start + u]
            g = grad_ref[:, :, lanes(col, block)].reshape(zc * tok_rows, block)
            prod = jnp.dot(flip_ref[0, row], g, preferred_element_type=F32)
            value = jnp.where(start + u < live, prod, 0.0)
            if steps == 1:
                out_ref[start + u] = value.astype(BF16)
            else:
                acc[start + u] = value + jnp.where(step == 0, 0.0, acc[start + u])

    def blank(slot, carry):
        if steps == 1:
            out_ref[slot] = jnp.zeros((block, block), BF16)
        else:
            acc[slot] = jnp.zeros((block, block), F32)
        return carry

    each_group(live, unroll, body)
    lax.fori_loop(live, own, blank, 0)
    if steps > 1:

        @pl.when(step == steps - 1)
        def _():
            out_ref[...] = acc[...].astype(BF16)


def on_device(
    zs, xs, hs, tokens, hidden_grad, gate_blocks, up_blocks, gate_rows, gate_cols, gate_count, up_rows, up_cols, up_count
):
    tok_rows, feat = tokens.shape
    width = hidden_grad.shape[1]
    own, block = gate_blocks.shape[1], gate_blocks.shape[2]
    per = feat // block
    unroll = math.gcd(own, 4)
    zc = math.gcd(zs, 4)
    steps = zs // zc
    many = zc * tok_rows
    zpos = lax.axis_index("z")
    xpos = lax.axis_index("x")
    flip_x = [(s, s ^ 1) for s in range(xs)]
    base = jnp.stack([(zpos * xs + xpos) * own, (zpos * xs + (xpos ^ 1)) * own]).astype(jnp.int32)
    gate_lists = (base, gate_count, gate_rows, gate_cols)
    up_lists = (base, up_count, up_rows, up_cols)
    smem = [pl.BlockSpec(memory_space=SMEM)] * 4
    block_spec = pl.BlockSpec((own, block, block), lambda i: (0, 0, 0))
    tok_spec = pl.BlockSpec((zc, hs, tok_rows, feat), lambda i: (i, 0, 0, 0))
    back_spec = pl.BlockSpec((hs, zc, tok_rows, feat), lambda i: (0, i, 0, 0))
    grad_spec = pl.BlockSpec((zc, tok_rows, width), lambda i: (i, 0, 0))
    flip_spec = pl.BlockSpec((1, hs * per, block, many), lambda i: (i, 0, 0, 0))
    params = pltpu.CompilerParams(vmem_limit_bytes=LIMIT)
    cost = pl.CostEstimate(flops=8 * zs * tok_rows * 2 * own * block * block, bytes_accessed=2**23, transcendentals=0)

    gate_mine, up_mine = gate_blocks[0], up_blocks[0]
    gate_other = lax.ppermute(gate_mine, "x", flip_x)
    up_other = lax.ppermute(up_mine, "x", flip_x)
    tok_all = lax.all_gather(tokens, ("z", "hid")).reshape(zs, hs, tok_rows, feat)

    def project(lists, mine, other):
        return pl.pallas_call(
            functools.partial(forward_kernel, own, block, per, unroll),
            grid=(steps,),
            in_specs=smem + [tok_spec, block_spec, block_spec],
            out_specs=grad_spec,
            out_shape=jax.ShapeDtypeStruct((zs, tok_rows, width), BF16),
            scratch_shapes=[VMEM((many, width + block), F32)],
            compiler_params=params,
            cost_estimate=cost,
        )(*lists, tok_all, mine, other)

    def bring_back(lists, grads, mine, other, prev):
        first = prev is None
        return pl.pallas_call(
            functools.partial(input_kernel, own, block, unroll, first),
            grid=(steps,),
            in_specs=smem + [grad_spec, block_spec, block_spec] + ([] if first else [back_spec]),
            out_specs=back_spec,
            out_shape=jax.ShapeDtypeStruct((hs, zs, tok_rows, feat), F32 if first else BF16),
            scratch_shapes=[VMEM((many, hs * feat + block), F32)],
            compiler_params=params,
            cost_estimate=cost,
        )(*lists, grads, mine, other, *(() if first else (prev,)))

    def weight_terms(lists, flipped, grads, half):
        return pl.pallas_call(
            functools.partial(weight_kernel, own, block, unroll, steps, half),
            grid=(steps,),
            in_specs=smem + [flip_spec, grad_spec],
            out_specs=block_spec,
            out_shape=jax.ShapeDtypeStruct((own, block, block), BF16),
            scratch_shapes=[VMEM((own if steps > 1 else 1, block, block), F32)],
            compiler_params=params,
            cost_estimate=cost,
        )(*lists, flipped, grads)

    gate_part = project(gate_lists, gate_mine, gate_other)
    up_part = project(up_lists, up_mine, up_other)
    later, _ = lax.optimization_barrier((tok_all, up_part))
    flipped = pl.pallas_call(
        functools.partial(flip_kernel, block, per),
        grid=(steps,),
        in_specs=[tok_spec],
        out_specs=flip_spec,
        out_shape=jax.ShapeDtypeStruct((steps, hs * per, block, many), BF16),
        compiler_params=params,
        cost_estimate=cost,
        name="flip",
    )(later)
    gate_pre = lax.psum_scatter(gate_part, "z", scatter_dimension=0, tiled=False).astype(F32)
    up_pre = lax.psum_scatter(up_part, "z", scatter_dimension=0, tiled=False).astype(F32)
    gate_pre, flipped = lax.optimization_barrier((gate_pre, flipped))
    sigma = jax.nn.sigmoid(gate_pre)
    activated = gate_pre * sigma
    slope = sigma * (1.0 + gate_pre * (1.0 - sigma))
    hidden = (activated * up_pre).astype(BF16)
    upstream = hidden_grad.astype(F32)
    gate_grad = lax.all_gather((upstream * up_pre * slope).astype(BF16), "z")
    up_grad = lax.all_gather((upstream * activated).astype(BF16), "z")

    back = bring_back(gate_lists, gate_grad, gate_mine, gate_other, None)
    gate_terms = weight_terms(gate_lists, flipped, gate_grad, 1)
    gate_kept = weight_terms(gate_lists, flipped, gate_grad, 0)
    back, gate_terms, gate_kept = lax.optimization_barrier((back, gate_terms, gate_kept))
    gate_sent = lax.ppermute(gate_terms, "x", flip_x)
    back = bring_back(up_lists, up_grad, up_mine, up_other, back)
    back = lax.psum_scatter(back, "hid", scatter_dimension=0, tiled=False)
    input_grad = lax.psum_scatter(back, "z", scatter_dimension=0, tiled=False)
    up_sent = lax.ppermute(weight_terms(up_lists, flipped, up_grad, 1), "x", flip_x)
    up_kept = weight_terms(up_lists, flipped, up_grad, 0)
    scale = 1.0 / math.sqrt(tok_rows * zs * xs)
    gate_out = ((gate_kept.astype(F32) + gate_sent.astype(F32)) * scale).astype(BF16)
    up_out = ((up_kept.astype(F32) + up_sent.astype(F32)) * scale).astype(BF16)
    return hidden, input_grad, gate_out[None], up_out[None]


def solution(mesh):
    seq, hid = mesh.shape["seq"], mesh.shape["hid"]
    xs = 2
    zs = seq // xs
    inner = Mesh(mesh.devices.reshape(zs, xs, hid), ("z", "x", "hid"))
    zx = ("z", "x")
    placed = (
        P(zx, "hid"),
        P(zx, "hid"),
        P("hid", zx, None, None),
        P("hid", zx, None, None),
        P("hid", None),
        P("hid", None),
        P("hid"),
        P("hid", None),
        P("hid", None),
        P("hid"),
    )
    return jax.shard_map(
        functools.partial(on_device, zs, xs, hid),
        mesh=inner,
        in_specs=placed,
        out_specs=(P(zx, "hid"), P(zx, "hid"), P("hid", zx, None, None), P("hid", zx, None, None)),
        check_vma=False,
    )
```

time: 1170 us -> 482 us (0.41)
  matrix products: 461 us -> 0 us
  local copies, waits for them, and re-layouts: 359 us -> 1.43 us
  waiting for transfers between devices: 240 us -> 341 us
  Pallas kernels: 0 us -> 93.8 us
  other arithmetic: 82.2 us -> 13.5 us
    dot_general x170 -> x0, matrix products: 461 us -> none  [the longest x56 213 us: place_split(): jnp.einsum(form, rest_part, table, preferred_element_type=jnp.float32)]
    convert_element_type x115 -> x0, local copies, waits for them, and re-layouts: 195 us -> none  [the longest x56 95.1 us: place_split(): high_part = products.astype(jnp.bfloat16)]
    gather x64 -> x0, local copies, waits for them, and re-layouts: 138 us -> none  [the longest x28 55.3 us: project_one_group(): picked = jnp.take(tiles, row_ids, axis=1)]
    reduce_scatter x1 -> x4, waiting for transfers between devices: 12.6 us -> 114 us  [the longest x1 69.8 us: on_device(): lax.psum_scatter(up_part, 'z', scatter_dimension=0, tiled=False).astype(F32)]
    all_gather x3, waiting for transfers between devices: 223 us -> 122 us  [the longest x1 71.9 us: on_device(): gate_grad = lax.all_gather((upstream * up_pre * slope).astype(BF16), 'z')]
    ppermute x5 -> x4, waiting for transfers between devices: 2.23 us -> 104 us  [the longest x1 39.1 us: on_device(): gate_other = lax.ppermute(gate_mine, 'x', flip_x)]
    pallas_call x0 -> x9, Pallas kernels: none -> 93.8 us  [the longest x4 31.6 us: weight_terms(): pl.pallas_call(functools.partial(weight_kernel, own, block, unroll, steps...]
    and x58 -> x0, other arithmetic: 40.6 us -> none  [the longest x28 20.3 us: project_one_group(): picked = jnp.take(tiles, row_ids, axis=1)]
  transfers between devices with their start and end apart: 9 -> 11, of which waited for: 5 -> 9; matrix products, arithmetic and copies ran while one was open for 71% -> 2% of each run, Pallas kernels for 0% -> 14%
where the time goes in v1:
time: 482 us; the launch traced here: 476 us
  waiting for transfers between devices  341 us (71%)
  Pallas kernels  93.8 us (19%)
  between operations  15.4 us (3%)
  other arithmetic  13.5 us (3%)
  starting transfers between devices  10.3 us (2%)
    all_gather x1, waiting for transfers between devices, on_device(): gate_grad = lax.all_gather((upstream * up_pre * slope).astype(BF16), 'z')  71.9 us
    reduce_scatter x1, waiting for transfers between devices, on_device(): lax.psum_scatter(up_part, 'z', scatter_dimension=0, tiled=False).astype(F32)  69.8 us
    ppermute x1, waiting for transfers between devices, on_device(): gate_other = lax.ppermute(gate_mine, 'x', flip_x)  39.1 us
    ppermute x1, waiting for transfers between devices, on_device(): up_other = lax.ppermute(up_mine, 'x', flip_x)  38.2 us
    all_gather x1, waiting for transfers between devices, on_device(): up_grad = lax.all_gather((upstream * activated).astype(BF16), 'z')  37.7 us
    reduce_scatter x1, waiting for transfers between devices, on_device(): back = lax.psum_scatter(back, 'hid', scatter_dimension=0, tiled=False)  36.9 us
    pallas_call x4, Pallas kernels, weight_terms(): pl.pallas_call(functools.partial(weight_kernel, own, block, unroll, steps...  31.6 us
    pallas_call x2, Pallas kernels, bring_back(): pl.pallas_call(functools.partial(input_kernel, own, block, unroll, first)...  29.4 us
  transfers between devices with their start and end apart: 11, of which 9 were waited for; matrix products, arithmetic and copies ran while one was open for 2% of the time, Pallas kernels for 14%

profile of v1, /device:TPU:0, one launch (start us, length us, event | category | flops | bytes accessed | tf_op | source)
XLA Modules:
  0.0 475.6 jit_solution(5016486799865686448)
XLA Ops:
  7.2 0.0 all-gather.7.cloned.1.call-start
  7.2 0.7 all-gather.7.cloned.1.call-update
  7.9 0.0 reduce-scatter.5.cloned.1.call-start
  7.9 3.0 collective-permute-start
  11.6 0.6 pad_add_fusion.base_ref
  12.2 39.1 %collective-permute-done.other_ref = bf16[56,128,128]{2,1,0:T(8,128)(2,1)} collective-permute-done((bf16[56,128,128]{2,1,0:T(8,128)(2,1)}, bf16[56,128,128]{2,1,0:T(8,128)(2,1)}, u32[]{:S(2)}, u32[]{:S(2)}) %collective-permute-start) | collective-permute-done | bytes 1835040 | tf_op jit(solution)/shard_map/ppermute | solution.py:155
  51.3 12.0 %all-gather.7.cloned.1.call-done = bf16[2048,1024]{1,0:T(8,128)(2,1)} async-done(((bf16[128,1024]{1,0:T(8,128)(2,1)}), bf16[2048,1024]{1,0:T(8,128)(2,1)}) %all-gather.7.cloned.1.call-update) | async-done | bytes 4194320 | tf_op jit(solution)/shard_map/all_gather | solution.py:157
  63.3 15.0 %shard_map.129 = bf16[4,128,3584]{2,1,0:T(8,128)(2,1)} custom-call(s32[2]{0:T(128)} %pad_add_fusion.base_ref, s32[1]{0:T(128)S(6)} %copy.14.live_ref, s32[1,448]{1,0:T(1,128)} %rows_ref.12, s32[1,448]{1,0:T(1,128)} %cols_ref.12, bf16[4,4,128,1024]{3,2,1,0:T(8,128)(2,1)} %bitcast.21, bf16[56,128,128]{2,1,0:T(8,128)(2,1)} %bitcast.31, ...), custom_call_target="tpu_custom_call" | custom-call | flops 7516192768 | bytes 8388608 | tf_op jit(solution)/shard_map/pallas_call | solution.py:160
  78.3 0.0 copy-start.2
  78.3 0.0 reduce-scatter.5.cloned.1.call-update
  78.3 0.0 reduce-scatter.7.cloned.1.call-start
  78.4 1.4 copy-done.2
  79.8 1.5 collective-permute-start.1
  81.9 38.2 %collective-permute-done.1.other_ref = bf16[56,128,128]{2,1,0:T(8,128)(2,1)} collective-permute-done((bf16[56,128,128]{2,1,0:T(8,128)(2,1)S(1)}, bf16[56,128,128]{2,1,0:T(8,128)(2,1)}, u32[]{:S(2)}, u32[]{:S(2)}) %collective-permute-start.1) | collective-permute-done | bytes 1835040 | tf_op jit(solution)/shard_map/ppermute | solution.py:156
  120.1 10.5 %shard_map.130 = bf16[4,128,3584]{2,1,0:T(8,128)(2,1)} custom-call(s32[2]{0:T(128)} %pad_add_fusion.base_ref, s32[1]{0:T(128)S(6)} %copy.15.live_ref, s32[1,448]{1,0:T(1,128)} %rows_ref.15, s32[1,448]{1,0:T(1,128)} %cols_ref.15, bf16[4,4,128,1024]{3,2,1,0:T(8,128)(2,1)} %bitcast.22, bf16[56,128,128]{2,1,0:T(8,128)(2,1)} %bitcast.33, ...), custom_call_target="tpu_custom_call" | custom-call | flops 7516192768 | bytes 8388608 | tf_op jit(solution)/shard_map/pallas_call | solution.py:160
  130.6 0.0 reduce-scatter.7.cloned.1.call-update
  130.6 0.0 all-gather.11.cloned.1.call-start
  130.7 7.2 %flip.1.flip_ref = bf16[1,32,128,512]{3,2,1,0:T(8,128)(2,1)} custom-call(bf16[4,4,128,1024]{3,2,1,0:T(8,128)(2,1)} %bitcast.23), custom_call_target="tpu_custom_call" | custom-call | flops 7516192768 | bytes 8388608 | tf_op jit(solution)/shard_map/flip/pallas_call | solution.py:199
  137.9 0.0 copy-start.1
  137.9 7.7 %reduce-scatter.5.cloned.1.call-done = bf16[1,128,3584]{2,1,0:T(8,128)(2,1)} async-done(((bf16[4,128,3584]{2,1,0:T(8,128)(2,1)}), bf16[1,128,3584]{2,1,0:T(8,128)(2,1)}) %reduce-scatter.5.cloned.1.call-update) | async-done | bytes 917520 | tf_op jit(solution)/shard_map/reduce_scatter | solution.py:209
  145.6 1.4 bitcast_convert_fusion
  146.9 69.8 %reduce-scatter.7.cloned.1.call-done = bf16[1,128,3584]{2,1,0:T(8,128)(2,1)} async-done(((bf16[4,128,3584]{2,1,0:T(8,128)(2,1)}), bf16[1,128,3584]{2,1,0:T(8,128)(2,1)}) %reduce-scatter.7.cloned.1.call-update) | async-done | bytes 917520 | tf_op jit(solution)/shard_map/reduce_scatter | solution.py:210
  216.7 0.0 copy-done.1
  216.7 3.7 fusion.3
  220.4 0.0 all-gather.11.cloned.1.call-update
  220.5 0.0 all-gather.9.cloned.1.call-start
  220.5 0.5 all-gather.9.cloned.1.call-update
  221.1 0.0 reduce-scatter.9.cloned.1.call-start
  221.1 71.9 %all-gather.11.cloned.1.call-done = bf16[512,3584]{1,0:T(8,128)(2,1)} async-done(((bf16[128,3584]{1,0:T(8,128)(2,1)}), bf16[512,3584]{1,0:T(8,128)(2,1)}) %all-gather.11.cloned.1.call-update) | async-done | bytes 3670032 | tf_op jit(solution)/shard_map/all_gather | solution.py:217
  293.0 8.9 %shard_map.133 = bf16[56,128,128]{2,1,0:T(8,128)(2,1)} custom-call(s32[2]{0:T(128)} %pad_add_fusion.base_ref, s32[1]{0:T(128)S(6)} %copy.14.live_ref, s32[1,448]{1,0:T(1,128)} %rows_ref.12, s32[1,448]{1,0:T(1,128)} %cols_ref.12, bf16[1,32,128,512]{3,2,1,0:T(8,128)(2,1)} %flip.1.flip_ref, bf16[4,128,3584]{2,1,0:T(8,128)(2,1)} %bitcast.27), custom_call_target="tpu_custom_call" | custom-call | flops 7516192768 | bytes 8388608 | tf_op jit(solution)/shard_map/pallas_call | solution.py:185
  301.9 9.0 %shard_map.132 = bf16[56,128,128]{2,1,0:T(8,128)(2,1)} custom-call(s32[2]{0:T(128)} %pad_add_fusion.base_ref, s32[1]{0:T(128)S(6)} %copy.14.live_ref, s32[1,448]{1,0:T(1,128)} %rows_ref.12, s32[1,448]{1,0:T(1,128)} %cols_ref.12, bf16[1,32,128,512]{3,2,1,0:T(8,128)(2,1)} %flip.1.flip_ref, bf16[4,128,3584]{2,1,0:T(8,128)(2,1)} %bitcast.28), custom_call_target="tpu_custom_call" | custom-call | flops 7516192768 | bytes 8388608 | tf_op jit(solution)/shard_map/pallas_call | solution.py:185
  310.9 16.5 %shard_map.131.rest_0_ = f32[4,4,128,1024]{3,2,1,0:T(8,128)} custom-call(s32[2]{0:T(128)} %pad_add_fusion.base_ref, s32[1]{0:T(128)S(6)} %copy.14.live_ref, s32[1,448]{1,0:T(1,128)} %rows_ref.12, s32[1,448]{1,0:T(1,128)} %cols_ref.12, bf16[4,128,3584]{2,1,0:T(8,128)(2,1)} %bitcast.29, bf16[56,128,128]{2,1,0:T(8,128)(2,1)} %bitcast.32, ...), custom_call_target="tpu_custom_call" | custom-call | flops 7516192768 | bytes 8388608 | tf_op jit(solution)/shard_map/pallas_call | solution.py:173
  327.4 37.7 %all-gather.9.cloned.1.call-done = bf16[512,3584]{1,0:T(8,128)(2,1)} async-done(((bf16[128,3584]{1,0:T(8,128)(2,1)}), bf16[512,3584]{1,0:T(8,128)(2,1)}) %all-gather.9.cloned.1.call-update) | async-done | bytes 3670032 | tf_op jit(solution)/shard_map/all_gather | solution.py:218
  365.1 12.9 %shard_map.134 = bf16[4,4,128,1024]{3,2,1,0:T(8,128)(2,1)} custom-call(s32[2]{0:T(128)} %pad_add_fusion.base_ref, s32[1]{0:T(128)S(6)} %copy.15.live_ref, s32[1,448]{1,0:T(1,128)} %rows_ref.15, s32[1,448]{1,0:T(1,128)} %cols_ref.15, bf16[4,128,3584]{2,1,0:T(8,128)(2,1)} %bitcast.24, bf16[56,128,128]{2,1,0:T(8,128)(2,1)} %bitcast.34, ...), custom_call_target="tpu_custom_call" | custom-call | flops 7516192768 | bytes 8388608 | tf_op jit(solution)/shard_map/pallas_call | solution.py:173
  378.0 0.0 reduce-scatter.9.cloned.1.call-update
  378.0 0.0 reduce-scatter.11.cloned.1.call-start
  378.1 4.9 %shard_map.136 = bf16[56,128,128]{2,1,0:T(8,128)(2,1)} custom-call(s32[2]{0:T(128)} %pad_add_fusion.base_ref, s32[1]{0:T(128)S(6)} %copy.15.live_ref, s32[1,448]{1,0:T(1,128)} %rows_ref.15, s32[1,448]{1,0:T(1,128)} %cols_ref.15, bf16[1,32,128,512]{3,2,1,0:T(8,128)(2,1)} %flip.1.flip_ref, bf16[4,128,3584]{2,1,0:T(8,128)(2,1)} %bitcast.25), custom_call_target="tpu_custom_call" | custom-call | flops 7516192768 | bytes 8388608 | tf_op jit(solution)/shard_map/pallas_call | solution.py:185
  383.0 5.5 %collective-permute-start.3 = (bf16[56,128,128]{2,1,0:T(8,128)(2,1)}, bf16[56,128,128]{2,1,0:T(8,128)(2,1)}, u32[]{:S(2)}, u32[]{:S(2)}) collective-permute-start(bf16[56,128,128]{2,1,0:T(8,128)(2,1)} %shard_map.136), channel_id=1, source_target_pairs={{0,4},{4,0},{1,5},{5,1},{2,6},{6,2},{3,7},{7,3},{8,12},{12,8},{9,1... | collective-permute-start | bytes 5505032 | tf_op jit(solution)/shard_map/ppermute | solution.py:228
  388.4 0.0 collective-permute-start.2
  388.4 36.9 %reduce-scatter.9.cloned.1.call-done = bf16[1,4,128,1024]{3,2,1,0:T(8,128)(2,1)} async-done(((bf16[4,4,128,1024]{3,2,1,0:T(8,128)(2,1)}), bf16[1,4,128,1024]{3,2,1,0:T(8,128)(2,1)}) %reduce-scatter.9.cloned.1.call-update) | async-done | bytes 1048592 | tf_op jit(solution)/shard_map/reduce_scatter | solution.py:226
  425.4 0.0 reduce-scatter.11.cloned.1.call-update
  425.4 8.9 %shard_map.135 = bf16[56,128,128]{2,1,0:T(8,128)(2,1)} custom-call(s32[2]{0:T(128)} %pad_add_fusion.base_ref, s32[1]{0:T(128)S(6)} %copy.15.live_ref, s32[1,448]{1,0:T(1,128)} %rows_ref.15, s32[1,448]{1,0:T(1,128)} %cols_ref.15, bf16[1,32,128,512]{3,2,1,0:T(8,128)(2,1)} %flip.1.flip_ref, bf16[4,128,3584]{2,1,0:T(8,128)(2,1)} %bitcast.26), custom_call_target="tpu_custom_call" | custom-call | flops 7516192768 | bytes 8388608 | tf_op jit(solution)/shard_map/pallas_call | solution.py:185
  434.3 0.0 copy-start
  434.3 0.0 collective-permute-done.3
  434.3 4.4 fusion.5
  438.7 26.6 %collective-permute-done.2 = bf16[56,128,128]{2,1,0:T(8,128)(2,1)} collective-permute-done((bf16[56,128,128]{2,1,0:T(8,128)(2,1)}, bf16[56,128,128]{2,1,0:T(8,128)(2,1)}, u32[]{:S(2)}, u32[]{:S(2)}) %collective-permute-start.2) | collective-permute-done | bytes 1835040 | tf_op jit(solution)/shard_map/ppermute | solution.py:224
  465.3 0.0 copy-done
  465.3 3.5 fusion.4
  468.8 0.0 reduce-scatter.11.cloned.1.call-done
Async XLA Ops:
  7.2 56.1 %all-gather.7.cloned.1.call-start = ((), (), s32[]{:S(2)}) async-start(), calls=%async_computation.8 | async-start | bytes 4456448 | tf_op jit(solution)/shard_map/all_gather | solution.py:157
  7.9 137.7 %reduce-scatter.5.cloned.1.call-start = ((), (), s32[]{:S(2)}) async-start(), calls=%async_computation.4 | async-start | bytes 4587520 | tf_op jit(solution)/shard_map/reduce_scatter | solution.py:209
  7.9 43.4 %collective-permute-start = (bf16[56,128,128]{2,1,0:T(8,128)(2,1)}, bf16[56,128,128]{2,1,0:T(8,128)(2,1)}, u32[]{:S(2)}, u32[]{:S(2)}) collective-permute-start(bf16[56,128,128]{2,1,0:T(8,128)(2,1)} %bitcast.30), channel_id=1, source_target_pairs={{0,4},{4,0},{1,5},{5,1},{2,6},{6,2},{3,7},{7,3},{8,12},{12,8},{9,1... | collective-permute-start | bytes 5505032 | tf_op jit(solution)/shard_map/ppermute | solution.py:155
  78.3 1.5 copy-start.2
  78.3 138.4 %reduce-scatter.7.cloned.1.call-start = ((), (), s32[]{:S(2)}) async-start(), calls=%async_computation.5 | async-start | bytes 4587520 | tf_op jit(solution)/shard_map/reduce_scatter | solution.py:210
  79.8 40.3 %collective-permute-start.1 = (bf16[56,128,128]{2,1,0:T(8,128)(2,1)S(1)}, bf16[56,128,128]{2,1,0:T(8,128)(2,1)}, u32[]{:S(2)}, u32[]{:S(2)}) collective-permute-start(bf16[56,128,128]{2,1,0:T(8,128)(2,1)S(1)} %bitcast.35), channel_id=1, source_target_pairs={{0,4},{4,0},{1,5},{5,1},{2,6},{6,2},{3,7},{7,3},{8,12},{12,8},{9,1... | collective-permute-start | bytes 5505032 | tf_op jit(solution)/shard_map/ppermute | solution.py:156
  130.6 162.3 %all-gather.11.cloned.1.call-start = ((), (), s32[]{:S(2)}) async-start(), calls=%async_computation.10 | async-start | bytes 4587520 | tf_op jit(solution)/shard_map/all_gather | solution.py:217
  137.9 78.9 %copy-start.1 = (bf16[128,3584]{1,0:T(8,128)(2,1)S(1)}, bf16[128,3584]{1,0:T(8,128)(2,1)}, u32[]{:S(2)}) copy-start(bf16[128,3584]{1,0:T(8,128)(2,1)} %param.11) | copy-start | bytes 2752516
  220.5 144.6 %all-gather.9.cloned.1.call-start = ((), (), s32[]{:S(2)}) async-start(), calls=%async_computation.9 | async-start | bytes 4587520 | tf_op jit(solution)/shard_map/all_gather | solution.py:218
  221.1 204.3 %reduce-scatter.9.cloned.1.call-start = ((), (), s32[]{:S(2)}) async-start(), calls=%async_computation.6 | async-start | bytes 5242880 | tf_op jit(solution)/shard_map/reduce_scatter | solution.py:226
  378.0 90.7 %reduce-scatter.11.cloned.1.call-start = ((), (), s32[]{:S(2)}) async-start(), calls=%async_computation.7 | async-start | bytes 1310720 | tf_op jit(solution)/shard_map/reduce_scatter | solution.py:227
  383.0 51.3 %collective-permute-start.3 = (bf16[56,128,128]{2,1,0:T(8,128)(2,1)}, bf16[56,128,128]{2,1,0:T(8,128)(2,1)}, u32[]{:S(2)}, u32[]{:S(2)}) collective-permute-start(bf16[56,128,128]{2,1,0:T(8,128)(2,1)} %shard_map.136), channel_id=1, source_target_pairs={{0,4},{4,0},{1,5},{5,1},{2,6},{6,2},{3,7},{7,3},{8,12},{12,8},{9,1... | collective-permute-start | bytes 5505032 | tf_op jit(solution)/shard_map/ppermute | solution.py:228
  388.4 76.9 %collective-permute-start.2 = (bf16[56,128,128]{2,1,0:T(8,128)(2,1)}, bf16[56,128,128]{2,1,0:T(8,128)(2,1)}, u32[]{:S(2)}, u32[]{:S(2)}) collective-permute-start(bf16[56,128,128]{2,1,0:T(8,128)(2,1)} %shard_map.132), channel_id=1, source_target_pairs={{0,4},{4,0},{1,5},{5,1},{2,6},{6,2},{3,7},{7,3},{8,12},{12,8},{9,1... | collective-permute-start | bytes 5505032 | tf_op jit(solution)/shard_map/ppermute | solution.py:224
  434.3 31.0 %copy-start = (bf16[56,128,128]{2,1,0:T(8,128)(2,1)S(1)}, bf16[56,128,128]{2,1,0:T(8,128)(2,1)}, u32[]{:S(2)}) copy-start(bf16[56,128,128]{2,1,0:T(8,128)(2,1)} %shard_map.133) | copy-start | bytes 5505028
Sparse Core Ops, SparseCore 0:
  10.1 53.0 all-gather.6
  78.4 67.0 reduce-scatter.4
  147.9 68.8 reduce-scatter.6
  220.6 72.3 all-gather.10
  294.4 70.6 all-gather.8
  378.1 47.1 reduce-scatter.8
  428.3 27.2 reduce-scatter.10
